TPU v7x, 256 devices: a whole 4x4x8 slice. The times are simulated.
256 devices in a mesh: layer: 8 (over y_lo, x), prow: 4 (over y_hi, core), pcol: 8 (over z).
Axes of the slice: x: 4, y: 4 (y_hi: 2, y_lo: 2; y = y_hi * 2 + y_lo), z: 8, core: 2. Of those that a mesh axis runs over, the one named last changes fastest.
Arguments:
- front_blocks: float32 [8, 4, 1024, 4, 1024], P('layer', None, 'prow', None, 'pcol'), may hold values from -6 to 6, as said below
- fill_mask: int32 [32, 32], replicated, may hold values from 0 to 1, as said below
Outputs:
- factored: float32 [8, 4, 1024, 4, 1024], P('layer', None, 'prow', None, 'pcol')
- ancestor: float32 [3, 4, 8, 32, 3, 1024], P(None, 'prow', 'layer', None, None, 'pcol')
Inputs may be any that keep to these rules, and one draw needn't show every extreme that they name: `front_blocks`: with the fill pattern applied, every pivot block that the elimination meets is invertible and well conditioned. `fill_mask`: block row i is filled exactly from some block column at most i // 2 through the diagonal block, and block column j exactly from some block row at most j // 2 through the diagonal block; all other block pairs are empty.
All inputs are finite; a program needn't handle non-finite values.
Results may differ from a plain program's by a relative error of at most 0.0001.
Values sent between devices are 32-bit elements; how exact they have to be, the bound alone decides.
A program may use at most 128 MiB of HBM per device.

v0:
```python
import jax
import jax.numpy as jnp
from jax import lax
from jax.sharding import Mesh
from jax.sharding import PartitionSpec as P

P_SIZE = 1024
BS = 128
PANELS = 1
PROW = ("prow_0", "prow_1")
PROW_PCOL = ("prow_0", "prow_1", "pcol")


def edges_of(length, count):
    lap = length // count
    if lap >= 8:
        lap -= lap % 8
    return [lap * k for k in range(1, count)]


def all_blocks(shard, axes, order):
    tiles = shard[None]
    for k in order:
        tiles = lax.all_gather(tiles, axes[k], axis=0, tiled=True)
    block = [lax.axis_size(axes[k]) for k in reversed(order)]
    tiles = tiles.reshape(*block, *shard.shape)
    turned = sorted(range(len(order)), key=lambda place: order[len(order) - 1 - place])
    return tiles.transpose(*turned, *range(len(order), tiles.ndim)).reshape(-1, *shard.shape)


def joined_along(tiles, dim):
    tiles = jnp.moveaxis(tiles, 0, dim)
    shape = tiles.shape
    return tiles.reshape(*shape[:dim], shape[dim] * shape[dim + 1], *shape[dim + 2 :])


def gather_all_axes(shard, axes, dim):
    numbers = list(range(len(axes)))[::-1]
    widest = shard.shape.index(max(shard.shape[:-1] or shard.shape))
    edges = [0, *edges_of(shard.shape[widest], len(axes)), shard.shape[widest]]
    finished = []
    for k, (start, end) in enumerate(zip(edges, edges[1:])):
        if end > start:
            share = lax.slice_in_dim(shard, start, end, axis=widest)
            finished.append(all_blocks(share, axes, numbers[k:] + numbers[:k]))
    return joined_along(jnp.concatenate(finished, axis=widest + 1), dim)


def sent_to_all(shard, axis):
    copies = jnp.broadcast_to(shard, (lax.axis_size(axis), *shard.shape))
    return lax.all_to_all(copies, axis, split_axis=0, concat_axis=0, tiled=True)


def gathered_copies(shard, axis, dim):
    tiles = sent_to_all(shard, axis)
    return joined_along(tiles, dim)


def cut_along(shard, dim, length):
    shape = shard.shape
    tiles = shard.reshape(*shape[:dim], length, shape[dim] // length, *shape[dim + 1 :])
    return jnp.moveaxis(tiles, dim, 0)


def summed_on_arrival(shard, axis, dim):
    length = lax.axis_size(axis)
    tiles = lax.all_to_all(cut_along(shard, dim, length), axis, 0, 0, tiled=True)
    return jnp.sum(tiles, axis=0)


def full_dot(left, right):
    return jnp.dot(left, right, precision=lax.Precision.HIGHEST, preferred_element_type=jnp.float32)


def invert(pivot_tile):
    gram_matrix = full_dot(pivot_tile.T, pivot_tile)
    cholesky_factor = jnp.linalg.cholesky(gram_matrix)
    return jax.scipy.linalg.cho_solve((cholesky_factor, True), pivot_tile.T)


def factor_pivot(matrix):
    pieces = []
    remainder = matrix
    for position in range(matrix.shape[0] // BS):
        pivot_tile = remainder[:BS, :BS]
        inverse = invert(pivot_tile)
        lower_part = full_dot(remainder[BS:, :BS], inverse)
        upper_part = remainder[:BS, BS:]
        pieces.append((pivot_tile, inverse, lower_part, upper_part))
        remainder = remainder[BS:, BS:] - full_dot(lower_part, upper_part)
    return pieces


def assemble(pieces):
    columns_list = []
    for column, piece in enumerate(pieces):
        above_part = [
            pieces[earlier][3][:, (column - earlier - 1) * BS : (column - earlier) * BS]
            for earlier in range(column)
        ]
        columns_list.append(jnp.concatenate(above_part + [piece[0], piece[2]], axis=0))
    return jnp.concatenate(columns_list, axis=1)


def solve_lower(row_data, pieces):
    results = []
    remaining_cols = row_data
    for pivot_tile, inverse, lower_part, upper_part in pieces:
        solved = full_dot(remaining_cols[:, :BS], inverse)
        results.append(solved)
        remaining_cols = remaining_cols[:, BS:] - full_dot(solved, upper_part)
    return jnp.concatenate(results, axis=1)


def solve_upper(column_data, pieces):
    results = []
    remaining_rows = column_data
    for pivot_tile, inverse, lower_part, upper_part in pieces:
        leading = remaining_rows[:BS]
        results.append(leading)
        remaining_rows = remaining_rows[BS:] - full_dot(lower_part, leading)
    return jnp.concatenate(results, axis=0)


def on_device(front_blocks, fill_mask):
    grid_row = lax.axis_index(PROW)
    grid_col = lax.axis_index("pcol")
    row_groups = lax.axis_size(PROW)
    col_groups = lax.axis_size("pcol")
    supers = front_blocks.shape[1]
    rows_dev = front_blocks.shape[2]
    cols_dev = front_blocks.shape[4]
    blocks_row = rows_dev // BS
    blocks_col = cols_dev // BS
    fill_table = fill_mask.reshape(supers, P_SIZE // BS, supers, P_SIZE // BS)
    fill_table = lax.dynamic_slice(
        fill_table,
        (0, grid_row * blocks_row, 0, grid_col * blocks_col),
        (supers, blocks_row, supers, blocks_col),
    )
    fill_table = jnp.broadcast_to(
        fill_table[:, :, None, :, :, None], (supers, blocks_row, BS, supers, blocks_col, BS)
    )
    fill_table = fill_table.reshape(supers, rows_dev, supers, cols_dev).astype(jnp.float32)
    current = front_blocks[0] * fill_table
    remaining = supers - 1
    own_tile = current[0, :, 0, :]
    gathered = gather_all_axes(own_tile[None], PROW_PCOL, 0)
    pivot_full = (
        gathered.reshape(row_groups, col_groups, rows_dev, cols_dev)
        .transpose(0, 2, 1, 3)
        .reshape(P_SIZE, P_SIZE)
    )
    pieces = factor_pivot(pivot_full)
    upper_rows = gathered_copies(current[0, :, 1:, :], PROW, 0)
    solved_upper = solve_upper(upper_rows.reshape(P_SIZE, remaining * cols_dev), pieces)
    below_part = current[1:, :, 0, :]
    widened = lax.all_gather(below_part, "pcol", axis=2, tiled=True)
    lower_rows = solve_lower(widened.reshape(remaining * rows_dev, P_SIZE), pieces).reshape(
        remaining, rows_dev, P_SIZE
    )
    factored_pivot = assemble(pieces)
    own_pivot = lax.dynamic_slice(
        factored_pivot, (grid_row * rows_dev, grid_col * cols_dev), (rows_dev, cols_dev)
    )
    own_upper = lax.dynamic_slice_in_dim(solved_upper, grid_row * rows_dev, rows_dev, 0).reshape(
        rows_dev, remaining, cols_dev
    )
    own_lower = lax.dynamic_slice_in_dim(lower_rows, grid_col * cols_dev, cols_dev, 2)
    update_term = full_dot(lower_rows.reshape(remaining * rows_dev, P_SIZE), solved_upper)
    trailing = current[1:, :, 1:, :] - update_term.reshape(remaining, rows_dev, remaining, cols_dev)
    current = current.at[0, :, 0, :].set(own_pivot)
    current = current.at[0, :, 1:, :].set(own_upper)
    current = current.at[1:, :, 0, :].set(own_lower)
    current = current.at[1:, :, 1:, :].set(trailing)
    trailing_own = current[PANELS:, :, PANELS:, :]
    summed = summed_on_arrival(trailing_own, "layer", 1)
    ancestor_rows = summed.shape[1]
    ancestor_part = summed.reshape(supers - PANELS, 1, 1, ancestor_rows, supers - PANELS, cols_dev)
    return (current[None], ancestor_part)


def solution(mesh):
    torus = Mesh(
        mesh.devices.reshape(mesh.shape["layer"], 2, 2, mesh.shape["pcol"]),
        ("layer", "prow_0", "prow_1", "pcol"),
    )
    placed = (P("layer", None, PROW, None, "pcol"), P())
    return jax.shard_map(
        on_device,
        mesh=torus,
        in_specs=placed,
        out_specs=(
            P("layer", None, PROW, None, "pcol"),
            P(None, PROW, "layer", None, None, "pcol"),
        ),
        check_vma=False,
    )
```

profile of v0, /device:TPU:16, one launch (start us, length us, event | category | flops | bytes accessed | tf_op | source)
XLA Modules:
  0.0 525.2 jit_solution(7103626663641285439)
XLA Ops:
  12.7 28.7 %all-gather = f32[8,80,128]{2,1,0:T(8,128)S(1)} all-gather(f32[1,80,128]{2,1,0:T(8,128)S(1)} %copy.66), channel_id=2, replica_groups=mesh['layer'=8,'prow_0'=2,'prow_1'=2,'pcol'=8] {'pcol'}, dimensions={0}, use_global_device_ids=true | all-gather | bytes 368640 | tf_op jit(solution)/shard_map/all_gather | solution.py:24
  44.1 6.3 %all-gather.6 = f32[2,96,128]{2,1,0:T(8,128)S(1)} all-gather(f32[1,96,128]{2,1,0:T(8,128)S(1)} %copy.69), channel_id=8, replica_groups=mesh['layer'=8,'prow_0'=2,'prow_1'=2,'pcol'=8] {'prow_0'}, dimensions={0}, use_global_device_ids=true | all-gather | bytes 147456 | tf_op jit(solution)/shard_map/all_gather | solution.py:24
  50.3 28.1 %all-gather.7 = f32[16,96,128]{2,1,0:T(8,128)} all-gather(f32[2,96,128]{2,1,0:T(8,128)S(1)} %all-gather.6), channel_id=9, replica_groups=mesh['layer'=8,'prow_0'=2,'prow_1'=2,'pcol'=8] {'pcol'}, dimensions={0}, use_global_device_ids=true | all-gather | bytes 884736 | tf_op jit(solution)/shard_map/all_gather | solution.py:24
  80.4 6.8 %all-gather.4 = f32[4,80,128]{2,1,0:T(8,128)} all-gather(f32[2,80,128]{2,1,0:T(8,128)S(1)} %all-gather.3), channel_id=6, replica_groups=mesh['layer'=8,'prow_0'=2,'prow_1'=2,'pcol'=8] {'prow_0'}, dimensions={0}, use_global_device_ids=true | all-gather | bytes 245760 | tf_op jit(solution)/shard_map/all_gather | solution.py:24
  88.6 4.8 all-to-all-start
  96.2 15.7 %all-to-all-done = f32[4,256,3,128]{1,3,2,0:T(8,128)} async-done(((f32[4,256,3,128]{1,3,2,0:T(8,128)}), f32[4,256,3,128]{1,3,2,0:T(8,128)}, u32[]{:S(2)}, u32[]{:S(2)}) %all-to-all-start) | async-done | bytes 1572896 | tf_op jit(solution)/shard_map/all_to_all | solution.py:51
  120.1 15.3 %all-gather.17.cloned.1.call-done = f32[32,80,128]{2,1,0:T(8,128)} async-done(((f32[4,80,128]{2,1,0:T(8,128)}), f32[32,80,128]{2,1,0:T(8,128)}) %all-gather.17.cloned.1.call-update) | async-done | bytes 1310736 | tf_op jit(solution)/shard_map/all_gather | solution.py:24
  141.1 11.7 %cholesky.134 = f32[128,128]{1,0:T(8,128)S(1)} custom-call(f32[128,128]{1,0:T(8,128)S(1)} %fusion.103), custom_call_target="Cholesky" | custom-call | tf_op jit(solution)/shard_map/jit(cholesky)/cholesky | solution.py:77
  154.2 9.8 %custom-call.14 = f32[1,128,128]{1,2,0:T(8,128)S(1)} custom-call(f32[1,128,128]{2,1,0:T(8,128)S(1)} %fusion.46), custom_call_target="InvertDiagBlocksLowerTriangular" | custom-call | tf_op jit(solution)/shard_map/jit(_cho_solve)/triangular_solve | solution.py:78
  168.3 5.2 slice_subtract_fusion
  175.8 11.7 %cholesky.145 = f32[128,128]{1,0:T(8,128)S(1)} custom-call(f32[128,128]{1,0:T(8,128)S(1)} %fusion.97), custom_call_target="Cholesky" | custom-call | tf_op jit(solution)/shard_map/jit(cholesky)/cholesky | solution.py:77
  188.8 9.8 %custom-call.15 = f32[1,128,128]{1,2,0:T(8,128)S(1)} custom-call(f32[1,128,128]{2,1,0:T(8,128)S(1)} %fusion.47), custom_call_target="InvertDiagBlocksLowerTriangular" | custom-call | tf_op jit(solution)/shard_map/jit(_cho_solve)/triangular_solve | solution.py:78
  205.4 11.9 %cholesky.156 = f32[128,128]{1,0:T(8,128)S(1)} custom-call(f32[128,128]{1,0:T(8,128)S(1)} %fusion.91), custom_call_target="Cholesky" | custom-call | tf_op jit(solution)/shard_map/jit(cholesky)/cholesky | solution.py:77
  218.7 9.8 %custom-call.16 = f32[1,128,128]{1,2,0:T(8,128)S(1)} custom-call(f32[1,128,128]{2,1,0:T(8,128)S(1)} %fusion.48), custom_call_target="InvertDiagBlocksLowerTriangular" | custom-call | tf_op jit(solution)/shard_map/jit(_cho_solve)/triangular_solve | solution.py:78
  231.9 3.0 slice_subtract_fusion.5
  246.8 13.2 %cholesky.167 = f32[128,128]{1,0:T(8,128)} custom-call(f32[128,128]{1,0:T(8,128)} %fusion.85), custom_call_target="Cholesky" | custom-call | tf_op jit(solution)/shard_map/jit(cholesky)/cholesky | solution.py:77
  263.7 11.4 %custom-call.17 = f32[1,128,128]{1,2,0:T(8,128)} custom-call(f32[1,128,128]{2,1,0:T(8,128)} %fusion.49), custom_call_target="InvertDiagBlocksLowerTriangular" | custom-call | tf_op jit(solution)/shard_map/jit(_cho_solve)/triangular_solve | solution.py:78
  291.6 13.2 %cholesky.178 = f32[128,128]{1,0:T(8,128)} custom-call(f32[128,128]{1,0:T(8,128)} %fusion.79), custom_call_target="Cholesky" | custom-call | tf_op jit(solution)/shard_map/jit(cholesky)/cholesky | solution.py:77
  308.4 11.3 %custom-call.18 = f32[1,128,128]{1,2,0:T(8,128)} custom-call(f32[1,128,128]{2,1,0:T(8,128)} %fusion.50), custom_call_target="InvertDiagBlocksLowerTriangular" | custom-call | tf_op jit(solution)/shard_map/jit(_cho_solve)/triangular_solve | solution.py:78
  333.3 12.1 %cholesky.189 = f32[128,128]{1,0:T(8,128)S(1)} custom-call(f32[128,128]{1,0:T(8,128)S(1)} %fusion.73), custom_call_target="Cholesky" | custom-call | tf_op jit(solution)/shard_map/jit(cholesky)/cholesky | solution.py:77
  346.8 9.8 %custom-call.19 = f32[1,128,128]{1,2,0:T(8,128)S(1)} custom-call(f32[1,128,128]{2,1,0:T(8,128)S(1)} %fusion.51), custom_call_target="InvertDiagBlocksLowerTriangular" | custom-call | tf_op jit(solution)/shard_map/jit(_cho_solve)/triangular_solve | solution.py:78
  369.6 12.5 %cholesky.200 = f32[128,128]{1,0:T(8,128)S(1)} custom-call(f32[128,128]{1,0:T(8,128)} %fusion.67), custom_call_target="Cholesky" | custom-call | tf_op jit(solution)/shard_map/jit(cholesky)/cholesky | solution.py:77
  384.3 10.6 %custom-call.20 = f32[1,128,128]{1,2,0:T(8,128)S(1)} custom-call(f32[1,128,128]{2,1,0:T(8,128)} %fusion.52), custom_call_target="InvertDiagBlocksLowerTriangular" | custom-call | tf_op jit(solution)/shard_map/jit(_cho_solve)/triangular_solve | solution.py:78
  423.7 11.7 %cholesky.211 = f32[128,128]{1,0:T(8,128)S(1)} custom-call(f32[128,128]{1,0:T(8,128)S(1)} %fusion.61), custom_call_target="Cholesky" | custom-call | tf_op jit(solution)/shard_map/jit(cholesky)/cholesky | solution.py:77
  436.7 10.0 %custom-call.21 = f32[1,128,128]{1,2,0:T(8,128)S(1)} custom-call(f32[1,128,128]{2,1,0:T(8,128)S(1)} %fusion.53), custom_call_target="InvertDiagBlocksLowerTriangular" | custom-call | tf_op jit(solution)/shard_map/jit(_cho_solve)/triangular_solve | solution.py:78
  449.3 3.5 copy.84
  454.4 4.5 slice_subtract_fusion.1
  459.4 3.2 slice_subtract_fusion.2
  479.3 7.5 %fusion.131 = f32[768,384]{1,0:T(8,128)} fusion(f32[768,1024]{0,1:T(8,128)S(1)} %convolution_dynamic-update-slice_fusion, f32[1024,384]{1,0:T(8,128)} %copy-done.16), kind=kOutput, calls=%fused_computation.254 | convolution fusion | flops 3623878656 | bytes 5898240 | tf_op jit(solution)/shard_map/dot_general | solution.py:72
  488.7 2.9 reshape.233
  499.6 4.9 all-to-all-start.1
  506.4 11.1 %all-to-all-done.1 = f32[8,3,32,3,128]{4,2,3,1,0:T(8,128)S(1)} async-done(((f32[8,3,32,3,128]{4,2,3,1,0:T(8,128)}), f32[8,3,32,3,128]{4,2,3,1,0:T(8,128)S(1)}, u32[]{:S(2)}, u32[]{:S(2)}) %all-to-all-start.1) | async-done | bytes 1179680 | tf_op jit(solution)/shard_map/all_to_all | solution.py:67
  (287 shorter events, 177.7 us)
Async XLA Ops:
  7.2 108.8 %all-gather.15.cloned.1.call-start = ((), (), s32[]{:S(2)}) async-start(), calls=%async_computation.2 | async-start | bytes 1966080 | tf_op jit(solution)/shard_map/all_gather | solution.py:24
  12.5 81.7 %copy-start = (f32[4,256,4,128]{1,3,2,0:T(8,128)}, f32[4,256,4,128]{1,3,2,0:T(8,128)S(1)}, u32[]{:S(2)}) copy-start(f32[4,256,4,128]{1,3,2,0:T(8,128)S(1)} %bitcast_multiply_fusion) | copy-start | bytes 6291460
  43.8 73.9 %all-gather.19.cloned.1.call-start = ((), (), s32[]{:S(2)}) async-start(), calls=%async_computation.4 | async-start | bytes 2359296 | tf_op jit(solution)/shard_map/all_gather | solution.py:24
  78.4 57.0 %all-gather.17.cloned.1.call-start = ((), (), s32[]{:S(2)}) async-start(), calls=%async_computation.3 | async-start | bytes 1474560 | tf_op jit(solution)/shard_map/all_gather | solution.py:24
  88.6 23.3 %all-to-all-start = ((f32[4,256,3,128]{1,3,2,0:T(8,128)}), f32[4,256,3,128]{1,3,2,0:T(8,128)}, u32[]{:S(2)}, u32[]{:S(2)}) async-start(f32[4,256,3,128]{1,3,2,0:T(8,128)} %broadcast_in_dim.36), calls=%async_computation | async-start | bytes 3145728 | tf_op jit(solution)/shard_map/all_to_all | solution.py:51
  93.4 356.0 %all-gather.21.cloned.1.call-start = ((), (), s32[]{:S(2)}) async-start(), calls=%async_computation.5 | async-start | bytes 3538944 | tf_op jit(solution)/shard_map/all_gather | solution.py:158
  173.5 151.9 %copy-start.5 = (f32[896,896]{1,0:T(8,128)}, f32[896,896]{1,0:T(8,128)S(1)}, u32[]{:S(2)}) copy-start(f32[896,896]{1,0:T(8,128)S(1)} %slice_subtract_fusion) | copy-start | bytes 9633796
  198.7 5.8 %copy-start.7 = (f32[896,128]{1,0:T(8,128)S(1)}, f32[896,128]{1,0:T(8,128)}, u32[]{:S(2)}) copy-start(f32[896,128]{1,0:T(8,128)} %copy-done.6) | copy-start | bytes 1376260
  200.3 4.2 copy-start.10
  228.5 6.4 %copy-start.11 = (f32[768,128]{1,0:T(8,128)S(1)}, f32[768,128]{1,0:T(8,128)}, u32[]{:S(2)}) copy-start(f32[768,128]{1,0:T(8,128)} %copy-done.10) | copy-start | bytes 1179652
  228.5 8.3 %copy-start.43 = (f32[128,128]{1,0:T(8,128)S(1)}, f32[128,128]{1,0:T(8,128)}, u32[]{:S(2)}) copy-start(f32[128,128]{1,0:T(8,128)} %slice.541) | copy-start | bytes 196612
  234.9 8.2 %copy-start.13 = (f32[640,640]{1,0:T(8,128)}, f32[640,640]{1,0:T(8,128)S(1)}, u32[]{:S(2)}) copy-start(f32[640,640]{1,0:T(8,128)S(1)} %slice_subtract_fusion.5) | copy-start | bytes 4915204
  277.4 7.2 %copy-start.36 = (f32[128,128]{1,0:T(8,128)}, f32[128,128]{1,0:T(8,128)S(1)}, u32[]{:S(2)}) copy-start(f32[128,128]{1,0:T(8,128)S(1)} %fusion.82) | copy-start | bytes 196612
  279.4 5.1 copy-start.19
  321.9 8.6 %copy-start.26 = (f32[128,128]{1,0:T(8,128)}, f32[128,128]{1,0:T(8,128)S(1)}, u32[]{:S(2)}) copy-start(f32[128,128]{1,0:T(8,128)S(1)} %fusion.76) | copy-start | bytes 196612
  323.9 6.6 %copy-start.22 = (f32[384,128]{1,0:T(8,128)}, f32[384,128]{1,0:T(8,128)S(1)}, u32[]{:S(2)}) copy-start(f32[384,128]{1,0:T(8,128)S(1)} %get-tuple-element.70) | copy-start | bytes 589828
  332.3 81.1 %copy-start.17 = (f32[384,384]{1,0:T(8,128)}, f32[384,384]{1,0:T(8,128)S(1)}, u32[]{:S(2)}) copy-start(f32[384,384]{1,0:T(8,128)S(1)} %convolution_subtract_fusion.8) | copy-start | bytes 1769476
  332.3 80.2 %copy-start.2 = (f32[4,256,4,128]{1,3,2,0:T(8,128)S(1)}, f32[4,256,4,128]{1,3,2,0:T(8,128)}, u32[]{:S(2)}) copy-start(f32[4,256,4,128]{1,3,2,0:T(8,128)} %copy-done) | copy-start | bytes 6291460
  357.1 40.0 %copy-start.28 = (f32[128,128]{1,0:T(8,128)}, f32[128,128]{1,0:T(8,128)S(1)}, u32[]{:S(2)}) copy-start(f32[128,128]{1,0:T(8,128)S(1)} %fusion.70) | copy-start | bytes 196612
  358.1 39.0 %copy-start.24 = (f32[256,128]{1,0:T(8,128)}, f32[256,128]{1,0:T(8,128)S(1)}, u32[]{:S(2)}) copy-start(f32[256,128]{1,0:T(8,128)S(1)} %get-tuple-element.72) | copy-start | bytes 393220
  366.5 30.6 %copy-start.21 = (f32[256,256]{1,0:T(8,128)}, f32[256,256]{1,0:T(8,128)S(1)}, u32[]{:S(2)}) copy-start(f32[256,256]{1,0:T(8,128)S(1)} %convolution_subtract_fusion.11) | copy-start | bytes 786436
  397.1 10.4 %copy-start.30 = (f32[128,128]{1,0:T(8,128)}, f32[128,128]{1,0:T(8,128)S(1)}, u32[]{:S(2)}) copy-start(f32[128,128]{1,0:T(8,128)S(1)} %fusion.64) | copy-start | bytes 196612
  398.0 9.6 %copy-start.38 = (f32[128,128]{1,0:T(8,128)}, f32[128,128]{1,0:T(8,128)S(1)}, u32[]{:S(2)}) copy-start(f32[128,128]{1,0:T(8,128)S(1)} %get-tuple-element.74) | copy-start | bytes 196612
  398.0 16.8 %copy-start.8 = (f32[896,128]{1,0:T(8,128)S(1)}, f32[896,128]{1,0:T(8,128)}, u32[]{:S(2)}) copy-start(f32[896,128]{1,0:T(8,128)} %copy-done.6) | copy-start | bytes 1376260
  413.4 4.1 copy-start.12
  414.8 4.9 copy-start.20
  454.4 4.5 copy-start.33
  466.5 5.1 copy-start.29
  469.5 4.7 copy-start.31
  488.7 6.3 %copy-start.1 = (f32[4,256,4,128]{1,3,2,0:T(8,128)S(1)}, f32[4,256,4,128]{1,3,2,0:T(8,128)}, u32[]{:S(2)}) copy-start(f32[4,256,4,128]{1,3,2,0:T(8,128)} %copy-done) | copy-start | bytes 6291460
  496.7 7.8 %copy-start.4 = (f32[1,4,256,4,128]{2,4,3,1,0:T(8,128)S(1)}, f32[1,4,256,4,128]{2,4,3,1,0:T(8,128)}, u32[]{:S(2)}) copy-start(f32[1,4,256,4,128]{2,4,3,1,0:T(8,128)} %get-tuple-element.58) | copy-start | bytes 6291460
  499.6 17.8 %all-to-all-start.1 = ((f32[8,3,32,3,128]{4,2,3,1,0:T(8,128)}), f32[8,3,32,3,128]{4,2,3,1,0:T(8,128)S(1)}, u32[]{:S(2)}, u32[]{:S(2)}) async-start(f32[8,3,32,3,128]{4,2,3,1,0:T(8,128)} %copy.90), calls=%async_computation.1 | async-start | bytes 2359296 | tf_op jit(solution)/shard_map/all_to_all | solution.py:67
  (20 other events, 41.6 us)
Sparse Core Ops, SparseCore 0:
  44.0 27.1 all-gather.14
  78.5 14.1 all-gather.18
  94.5 40.8 all-gather.16
  137.1 43.7 all-gather.20
where the time goes:
time: 531 us; the launch traced here: 525 us
  other arithmetic  214 us (40%)
  local copies, waits for them, and re-layouts  92.3 us (17%)
  matrix products  77.4 us (15%)
  blocking collectives  74.1 us (14%)
  waiting for transfers between devices  42.2 us (8%)
  between operations  15.5 us (3%)
  starting transfers between devices  9.82 us (2%)
    another operation x24, other arithmetic, invert(): cholesky_factor = jnp.linalg.cholesky(gram_matrix)  105 us
    another operation x16, other arithmetic, invert(): return jax.scipy.linalg.cho_solve((cholesky_factor, True), pivot_tile.T)  91.4 us
    all_gather x6, blocking collectives, all_blocks(): tiles = lax.all_gather(tiles, axes[k], axis=0, tiled=True)  74.1 us
    dot_general x45, matrix products, full_dot(): jnp.dot(left, right, precision=lax.Precision.HIGHEST, preferred_element_t...  67.3 us
    unnamed x134, local copies, waits for them, and re-layouts  52.4 us
    all_to_all x1, waiting for transfers between devices, sent_to_all(): return lax.all_to_all(copies, axis, split_axis=0, concat_axis=0, tiled=True)  15.7 us
    all_gather x3, waiting for transfers between devices, all_blocks(): tiles = lax.all_gather(tiles, axes[k], axis=0, tiled=True)  15.3 us
    all_to_all x1, waiting for transfers between devices, summed_on_arrival(): lax.all_to_all(cut_along(shard, dim, length), axis, 0, 0, tiled=True)  11.1 us
  transfers between devices with their start and end apart: 6, of which 3 were waited for; matrix products, arithmetic and copies ran while one was open for 61% of the time, Pallas kernels for 0%

commit v1 on v0

--- a/solution.py
+++ b/solution.py
@@ -11,6 +11,11 @@
 PROW_PCOL = ("prow_0", "prow_1", "pcol")
 
 
+def swapped_in(x, axis, dim):
+    stack = jnp.stack([x] * lax.axis_size(axis))
+    return jnp.concatenate(lax.all_to_all(stack, axis, 0, 0), axis=dim)
+
+
 def edges_of(length, count):
     lap = length // count
     if lap >= 8:
@@ -21,7 +26,7 @@
 def all_blocks(shard, axes, order):
     tiles = shard[None]
     for k in order:
-        tiles = lax.all_gather(tiles, axes[k], axis=0, tiled=True)
+        tiles = swapped_in(tiles, axes[k], 0)
     block = [lax.axis_size(axes[k]) for k in reversed(order)]
     tiles = tiles.reshape(*block, *shard.shape)
     turned = sorted(range(len(order)), key=lambda place: order[len(order) - 1 - place])

time: 531 us -> 593 us (1.12)
  waiting for transfers between devices: 42.2 us -> 112 us
  blocking collectives: 74.1 us -> 12.8 us
  starting transfers between devices: 9.82 us -> 50.9 us
  other arithmetic: 214 us -> 220 us
    all_to_all x0 -> x7, waiting for transfers between devices: none -> 80 us  [swapped_in(): return jnp.concatenate(lax.all_to_all(stack, axis, 0, 0), axis=dim)]
    all_gather x6 -> x0, blocking collectives: 74.1 us -> none  [all_blocks(): tiles = lax.all_gather(tiles, axes[k], axis=0, tiled=True)]
    all_to_all x0 -> x7, starting transfers between devices: none -> 38 us  [swapped_in(): return jnp.concatenate(lax.all_to_all(stack, axis, 0, 0), axis=dim)]
    all_gather x3 -> x0, waiting for transfers between devices: 15.3 us -> none  [all_blocks(): tiles = lax.all_gather(tiles, axes[k], axis=0, tiled=True)]
    all_to_all x0 -> x2, blocking collectives: none -> 12.8 us  [swapped_in(): return jnp.concatenate(lax.all_to_all(stack, axis, 0, 0), axis=dim)]
    unnamed x134 -> x136, local copies, waits for them, and re-layouts: 52.4 us -> 52.7 us
  transfers between devices with their start and end apart: 6 -> 10, of which waited for: 3 -> 9; matrix products, arithmetic and copies ran while one was open for 61% -> 55% of each run, Pallas kernels for 0% -> 0%
where the time goes in v1:
time: 593 us; the launch traced here: 584 us
  other arithmetic  220 us (37%)
  waiting for transfers between devices  112 us (19%)
  local copies, waits for them, and re-layouts  94.6 us (16%)
  matrix products  77.2 us (13%)
  starting transfers between devices  50.9 us (9%)
  between operations  15.8 us (3%)
  blocking collectives  12.8 us (2%)
    another operation x24, other arithmetic, invert(): cholesky_factor = jnp.linalg.cholesky(gram_matrix)  105 us
    another operation x16, other arithmetic, invert(): return jax.scipy.linalg.cho_solve((cholesky_factor, True), pivot_tile.T)  91.4 us
    all_to_all x7, waiting for transfers between devices, swapped_in(): return jnp.concatenate(lax.all_to_all(stack, axis, 0, 0), axis=dim)  80 us
    dot_general x45, matrix products, full_dot(): jnp.dot(left, right, precision=lax.Precision.HIGHEST, preferred_element_t...  67.3 us
    unnamed x136, local copies, waits for them, and re-layouts  52.7 us
    all_to_all x7, starting transfers between devices, swapped_in(): return jnp.concatenate(lax.all_to_all(stack, axis, 0, 0), axis=dim)  38 us
    all_to_all x1, waiting for transfers between devices, sent_to_all(): return lax.all_to_all(copies, axis, split_axis=0, concat_axis=0, tiled=True)  17.2 us
    all_to_all x1, waiting for transfers between devices, summed_on_arrival(): lax.all_to_all(cut_along(shard, dim, length), axis, 0, 0, tiled=True)  14.9 us
  transfers between devices with their start and end apart: 10, of which 9 were waited for; matrix products, arithmetic and copies ran while one was open for 55% of the time, Pallas kernels for 0%

profile of v1, /device:TPU:16, one launch (start us, length us, event | category | flops | bytes accessed | tf_op | source)
XLA Modules:
  0.0 583.7 jit_solution(5743871851725914760)
XLA Ops:
  18.2 5.4 all-to-all-start.6
  26.6 7.9 %all-to-all-start = ((f32[8,1,1,80,128]{4,3,2,1,0:T(8,128)}), f32[8,1,1,80,128]{4,3,2,1,0:T(8,128)S(1)}, u32[]{:S(2)}, u32[]{:S(2)}) async-start(f32[8,1,1,80,128]{4,3,2,1,0:T(8,128)} %stack.27), calls=%async_computation | async-start | bytes 655360 | tf_op jit(solution)/shard_map/all_to_all | solution.py:16
  35.2 11.8 %all-to-all-done = f32[8,1,1,80,128]{4,3,2,1,0:T(8,128)S(1)} async-done(((f32[8,1,1,80,128]{4,3,2,1,0:T(8,128)}), f32[8,1,1,80,128]{4,3,2,1,0:T(8,128)S(1)}, u32[]{:S(2)}, u32[]{:S(2)}) %all-to-all-start) | async-done | bytes 327712 | tf_op jit(solution)/shard_map/all_to_all | solution.py:16
  47.0 6.7 %all-to-all-start.4 = ((f32[2,2,1,80,128]{4,3,2,1,0:T(8,128)}), f32[2,2,1,80,128]{4,3,2,1,0:T(8,128)S(1)}, u32[]{:S(2)}, u32[]{:S(2)}) async-start(f32[2,2,1,80,128]{4,3,2,1,0:T(8,128)} %maximum_bitcast_fusion.1), calls=%async_computation.4 | async-start | bytes 327680 | tf_op jit(solution)/shard_map/all_to_all | solution.py:16
  56.3 5.0 all_to_all.55
  65.9 23.6 %all-to-all-done.7 = f32[8,2,1,96,128]{4,3,1,2,0:T(8,128)S(1)} async-done(((f32[8,2,1,96,128]{4,3,1,2,0:T(8,128)}), f32[8,2,1,96,128]{4,3,1,2,0:T(8,128)S(1)}, u32[]{:S(2)}, u32[]{:S(2)}) %all-to-all-start.7) | async-done | bytes 786464 | tf_op jit(solution)/shard_map/all_to_all | solution.py:16
  90.8 7.8 %all-to-all-start.9 = ((f32[4,256,3,128]{1,3,2,0:T(8,128)}), f32[4,256,3,128]{1,3,2,0:T(8,128)}, u32[]{:S(2)}, u32[]{:S(2)}) async-start(f32[4,256,3,128]{1,3,2,0:T(8,128)} %broadcast_in_dim.24), calls=%async_computation.9 | async-start | bytes 3145728 | tf_op jit(solution)/shard_map/all_to_all | solution.py:56
  100.0 17.2 %all-to-all-done.9 = f32[4,256,3,128]{1,3,2,0:T(8,128)} async-done(((f32[4,256,3,128]{1,3,2,0:T(8,128)}), f32[4,256,3,128]{1,3,2,0:T(8,128)}, u32[]{:S(2)}, u32[]{:S(2)}) %all-to-all-start.9) | async-done | bytes 1572896 | tf_op jit(solution)/shard_map/all_to_all | solution.py:56
  117.1 7.8 %all_to_all.56 = f32[2,16,1,96,128]{4,3,1,2,0:T(8,128)} all-to-all(f32[2,16,1,96,128]{4,3,1,2,0:T(8,128)} %pad_maximum_fusion), channel_id=1, replica_groups=mesh['layer'=8,'prow_0'=2,'prow_1'=2,'pcol'=8] {'prow_1'}, dimensions={0} | all-to-all | bytes 3145728 | tf_op jit(solution)/shard_map/all_to_all | solution.py:16
  132.2 32.4 %all-to-all-done.5 = f32[8,4,1,80,128]{4,3,1,2,0:T(8,128)S(1)} async-done(((f32[8,4,1,80,128]{4,3,1,2,0:T(8,128)}), f32[8,4,1,80,128]{4,3,1,2,0:T(8,128)S(1)}, u32[]{:S(2)}, u32[]{:S(2)}) %all-to-all-start.5) | async-done | bytes 1310752 | tf_op jit(solution)/shard_map/all_to_all | solution.py:16
  164.5 7.7 %all-to-all-start.2 = ((f32[2,16,1,80,128]{4,3,1,2,0:T(8,128)}), f32[2,16,1,80,128]{4,3,1,2,0:T(8,128)}, u32[]{:S(2)}, u32[]{:S(2)}) async-start(f32[2,16,1,80,128]{4,3,1,2,0:T(8,128)} %pad_maximum_fusion.1), calls=%async_computation.2 | async-start | bytes 2621440 | tf_op jit(solution)/shard_map/all_to_all | solution.py:16
  180.6 6.9 %all-to-all-done.2 = f32[2,16,1,80,128]{4,3,1,2,0:T(8,128)} async-done(((f32[2,16,1,80,128]{4,3,1,2,0:T(8,128)}), f32[2,16,1,80,128]{4,3,1,2,0:T(8,128)}, u32[]{:S(2)}, u32[]{:S(2)}) %all-to-all-start.2) | async-done | bytes 1310752 | tf_op jit(solution)/shard_map/all_to_all | solution.py:16
  195.4 11.7 %cholesky.134 = f32[128,128]{1,0:T(8,128)S(1)} custom-call(f32[128,128]{1,0:T(8,128)S(1)} %fusion.103), custom_call_target="Cholesky" | custom-call | tf_op jit(solution)/shard_map/jit(cholesky)/cholesky | solution.py:82
  208.5 9.8 %custom-call.14 = f32[1,128,128]{1,2,0:T(8,128)S(1)} custom-call(f32[1,128,128]{2,1,0:T(8,128)S(1)} %fusion.46), custom_call_target="InvertDiagBlocksLowerTriangular" | custom-call | tf_op jit(solution)/shard_map/jit(_cho_solve)/triangular_solve | solution.py:83
  222.6 5.2 slice_subtract_fusion
  230.0 11.7 %cholesky.145 = f32[128,128]{1,0:T(8,128)S(1)} custom-call(f32[128,128]{1,0:T(8,128)S(1)} %fusion.97), custom_call_target="Cholesky" | custom-call | tf_op jit(solution)/shard_map/jit(cholesky)/cholesky | solution.py:82
  243.0 9.8 %custom-call.15 = f32[1,128,128]{1,2,0:T(8,128)S(1)} custom-call(f32[1,128,128]{2,1,0:T(8,128)S(1)} %fusion.47), custom_call_target="InvertDiagBlocksLowerTriangular" | custom-call | tf_op jit(solution)/shard_map/jit(_cho_solve)/triangular_solve | solution.py:83
  259.6 11.9 %cholesky.156 = f32[128,128]{1,0:T(8,128)S(1)} custom-call(f32[128,128]{1,0:T(8,128)S(1)} %fusion.91), custom_call_target="Cholesky" | custom-call | tf_op jit(solution)/shard_map/jit(cholesky)/cholesky | solution.py:82
  272.7 9.8 %custom-call.16 = f32[1,128,128]{1,2,0:T(8,128)S(1)} custom-call(f32[1,128,128]{2,1,0:T(8,128)S(1)} %fusion.48), custom_call_target="InvertDiagBlocksLowerTriangular" | custom-call | tf_op jit(solution)/shard_map/jit(_cho_solve)/triangular_solve | solution.py:83
  300.8 13.2 %cholesky.167 = f32[128,128]{1,0:T(8,128)} custom-call(f32[128,128]{1,0:T(8,128)} %fusion.85), custom_call_target="Cholesky" | custom-call | tf_op jit(solution)/shard_map/jit(cholesky)/cholesky | solution.py:82
  317.7 11.4 %custom-call.17 = f32[1,128,128]{1,2,0:T(8,128)} custom-call(f32[1,128,128]{2,1,0:T(8,128)} %fusion.49), custom_call_target="InvertDiagBlocksLowerTriangular" | custom-call | tf_op jit(solution)/shard_map/jit(_cho_solve)/triangular_solve | solution.py:83
  345.6 13.2 %cholesky.178 = f32[128,128]{1,0:T(8,128)} custom-call(f32[128,128]{1,0:T(8,128)} %fusion.79), custom_call_target="Cholesky" | custom-call | tf_op jit(solution)/shard_map/jit(cholesky)/cholesky | solution.py:82
  362.4 11.3 %custom-call.18 = f32[1,128,128]{1,2,0:T(8,128)} custom-call(f32[1,128,128]{2,1,0:T(8,128)} %fusion.50), custom_call_target="InvertDiagBlocksLowerTriangular" | custom-call | tf_op jit(solution)/shard_map/jit(_cho_solve)/triangular_solve | solution.py:83
  387.4 12.1 %cholesky.189 = f32[128,128]{1,0:T(8,128)S(1)} custom-call(f32[128,128]{1,0:T(8,128)S(1)} %fusion.73), custom_call_target="Cholesky" | custom-call | tf_op jit(solution)/shard_map/jit(cholesky)/cholesky | solution.py:82
  400.9 9.8 %custom-call.19 = f32[1,128,128]{1,2,0:T(8,128)S(1)} custom-call(f32[1,128,128]{2,1,0:T(8,128)S(1)} %fusion.51), custom_call_target="InvertDiagBlocksLowerTriangular" | custom-call | tf_op jit(solution)/shard_map/jit(_cho_solve)/triangular_solve | solution.py:83
  423.8 12.5 %cholesky.200 = f32[128,128]{1,0:T(8,128)S(1)} custom-call(f32[128,128]{1,0:T(8,128)} %fusion.67), custom_call_target="Cholesky" | custom-call | tf_op jit(solution)/shard_map/jit(cholesky)/cholesky | solution.py:82
  438.3 10.8 %custom-call.20 = f32[1,128,128]{1,2,0:T(8,128)S(1)} custom-call(f32[1,128,128]{2,1,0:T(8,128)} %fusion.52), custom_call_target="InvertDiagBlocksLowerTriangular" | custom-call | tf_op jit(solution)/shard_map/jit(_cho_solve)/triangular_solve | solution.py:83
  477.8 11.7 %cholesky.211 = f32[128,128]{1,0:T(8,128)S(1)} custom-call(f32[128,128]{1,0:T(8,128)S(1)} %fusion.61), custom_call_target="Cholesky" | custom-call | tf_op jit(solution)/shard_map/jit(cholesky)/cholesky | solution.py:82
  490.8 10.0 %custom-call.21 = f32[1,128,128]{1,2,0:T(8,128)S(1)} custom-call(f32[1,128,128]{2,1,0:T(8,128)S(1)} %fusion.53), custom_call_target="InvertDiagBlocksLowerTriangular" | custom-call | tf_op jit(solution)/shard_map/jit(_cho_solve)/triangular_solve | solution.py:83
  533.4 7.5 %fusion.130 = f32[768,384]{1,0:T(8,128)} fusion(f32[768,1024]{0,1:T(8,128)S(1)} %convolution_dynamic-update-slice_fusion, f32[1024,384]{1,0:T(8,128)} %copy-done.17), kind=kOutput, calls=%fused_computation.262 | convolution fusion | flops 3623878656 | bytes 5898240 | tf_op jit(solution)/shard_map/dot_general | solution.py:77
  553.9 5.1 all-to-all-start.10
  560.8 14.9 %all-to-all-done.10 = f32[8,3,32,3,128]{4,2,3,1,0:T(8,128)S(1)} async-done(((f32[8,3,32,3,128]{4,2,3,1,0:T(8,128)}), f32[8,3,32,3,128]{4,2,3,1,0:T(8,128)S(1)}, u32[]{:S(2)}, u32[]{:S(2)}) %all-to-all-start.10) | async-done | bytes 1179680 | tf_op jit(solution)/shard_map/all_to_all | solution.py:72
  (299 shorter events, 214.5 us)
Async XLA Ops:
  12.4 160.6 %copy-start = (f32[4,256,4,128]{1,3,2,0:T(8,128)}, f32[4,256,4,128]{1,3,2,0:T(8,128)S(1)}, u32[]{:S(2)}) copy-start(f32[4,256,4,128]{1,3,2,0:T(8,128)S(1)} %bitcast_multiply_fusion) | copy-start | bytes 6291460
  13.5 4.7 all-to-all-start.3
  18.2 7.7 %all-to-all-start.6 = ((f32[2,1,1,96,128]{4,3,2,1,0:T(8,128)}), f32[2,1,1,96,128]{4,3,2,1,0:T(8,128)S(1)}, u32[]{:S(2)}, u32[]{:S(2)}) async-start(f32[2,1,1,96,128]{4,3,2,1,0:T(8,128)} %copy.70), calls=%async_computation.6 | async-start | bytes 196608 | tf_op jit(solution)/shard_map/all_to_all | solution.py:16
  26.6 20.3 %all-to-all-start = ((f32[8,1,1,80,128]{4,3,2,1,0:T(8,128)}), f32[8,1,1,80,128]{4,3,2,1,0:T(8,128)S(1)}, u32[]{:S(2)}, u32[]{:S(2)}) async-start(f32[8,1,1,80,128]{4,3,2,1,0:T(8,128)} %stack.27), calls=%async_computation | async-start | bytes 655360 | tf_op jit(solution)/shard_map/all_to_all | solution.py:16
  47.0 9.3 %all-to-all-start.4 = ((f32[2,2,1,80,128]{4,3,2,1,0:T(8,128)}), f32[2,2,1,80,128]{4,3,2,1,0:T(8,128)S(1)}, u32[]{:S(2)}, u32[]{:S(2)}) async-start(f32[2,2,1,80,128]{4,3,2,1,0:T(8,128)} %maximum_bitcast_fusion.1), calls=%async_computation.4 | async-start | bytes 327680 | tf_op jit(solution)/shard_map/all_to_all | solution.py:16
  62.3 27.2 %all-to-all-start.7 = ((f32[8,2,1,96,128]{4,3,1,2,0:T(8,128)}), f32[8,2,1,96,128]{4,3,1,2,0:T(8,128)S(1)}, u32[]{:S(2)}, u32[]{:S(2)}) async-start(f32[8,2,1,96,128]{4,3,1,2,0:T(8,128)} %stack.34), calls=%async_computation.7 | async-start | bytes 1572864 | tf_op jit(solution)/shard_map/all_to_all | solution.py:16
  90.8 26.3 %all-to-all-start.9 = ((f32[4,256,3,128]{1,3,2,0:T(8,128)}), f32[4,256,3,128]{1,3,2,0:T(8,128)}, u32[]{:S(2)}, u32[]{:S(2)}) async-start(f32[4,256,3,128]{1,3,2,0:T(8,128)} %broadcast_in_dim.24), calls=%async_computation.9 | async-start | bytes 3145728 | tf_op jit(solution)/shard_map/all_to_all | solution.py:56
  126.1 38.4 %all-to-all-start.5 = ((f32[8,4,1,80,128]{4,3,1,2,0:T(8,128)}), f32[8,4,1,80,128]{4,3,1,2,0:T(8,128)S(1)}, u32[]{:S(2)}, u32[]{:S(2)}) async-start(f32[8,4,1,80,128]{4,3,1,2,0:T(8,128)} %stack.32), calls=%async_computation.5 | async-start | bytes 2621440 | tf_op jit(solution)/shard_map/all_to_all | solution.py:16
  164.5 22.9 %all-to-all-start.2 = ((f32[2,16,1,80,128]{4,3,1,2,0:T(8,128)}), f32[2,16,1,80,128]{4,3,1,2,0:T(8,128)}, u32[]{:S(2)}, u32[]{:S(2)}) async-start(f32[2,16,1,80,128]{4,3,1,2,0:T(8,128)} %pad_maximum_fusion.1), calls=%async_computation.2 | async-start | bytes 2621440 | tf_op jit(solution)/shard_map/all_to_all | solution.py:16
  172.2 331.3 %all-gather.3.cloned.1.call-start = ((), (), s32[]{:S(2)}) async-start(), calls=%async_computation.11 | async-start | bytes 3538944 | tf_op jit(solution)/shard_map/all_gather | solution.py:163
  227.7 151.7 %copy-start.5 = (f32[896,896]{1,0:T(8,128)}, f32[896,896]{1,0:T(8,128)S(1)}, u32[]{:S(2)}) copy-start(f32[896,896]{1,0:T(8,128)S(1)} %slice_subtract_fusion) | copy-start | bytes 9633796
  252.8 5.8 copy-start.7
  282.5 6.4 %copy-start.12 = (f32[768,128]{1,0:T(8,128)S(1)}, f32[768,128]{1,0:T(8,128)}, u32[]{:S(2)}) copy-start(f32[768,128]{1,0:T(8,128)} %copy-done.11) | copy-start | bytes 1179652
  282.5 8.3 %copy-start.44 = (f32[128,128]{1,0:T(8,128)S(1)}, f32[128,128]{1,0:T(8,128)}, u32[]{:S(2)}) copy-start(f32[128,128]{1,0:T(8,128)} %slice.544) | copy-start | bytes 196612
  288.9 8.2 %copy-start.14 = (f32[640,640]{1,0:T(8,128)}, f32[640,640]{1,0:T(8,128)S(1)}, u32[]{:S(2)}) copy-start(f32[640,640]{1,0:T(8,128)S(1)} %slice_subtract_fusion.5) | copy-start | bytes 4915204
  331.4 7.2 %copy-start.37 = (f32[128,128]{1,0:T(8,128)}, f32[128,128]{1,0:T(8,128)S(1)}, u32[]{:S(2)}) copy-start(f32[128,128]{1,0:T(8,128)S(1)} %fusion.82) | copy-start | bytes 196612
  333.4 5.2 copy-start.20
  375.9 8.6 %copy-start.27 = (f32[128,128]{1,0:T(8,128)}, f32[128,128]{1,0:T(8,128)S(1)}, u32[]{:S(2)}) copy-start(f32[128,128]{1,0:T(8,128)S(1)} %fusion.76) | copy-start | bytes 196612
  377.9 6.6 %copy-start.23 = (f32[384,128]{1,0:T(8,128)}, f32[384,128]{1,0:T(8,128)S(1)}, u32[]{:S(2)}) copy-start(f32[384,128]{1,0:T(8,128)S(1)} %get-tuple-element.70) | copy-start | bytes 589828
  386.3 81.1 %copy-start.18 = (f32[384,384]{1,0:T(8,128)}, f32[384,384]{1,0:T(8,128)S(1)}, u32[]{:S(2)}) copy-start(f32[384,384]{1,0:T(8,128)S(1)} %convolution_subtract_fusion.8) | copy-start | bytes 1769476
  386.3 80.2 %copy-start.2 = (f32[4,256,4,128]{1,3,2,0:T(8,128)S(1)}, f32[4,256,4,128]{1,3,2,0:T(8,128)}, u32[]{:S(2)}) copy-start(f32[4,256,4,128]{1,3,2,0:T(8,128)} %copy-done) | copy-start | bytes 6291460
  411.2 39.9 %copy-start.29 = (f32[128,128]{1,0:T(8,128)}, f32[128,128]{1,0:T(8,128)S(1)}, u32[]{:S(2)}) copy-start(f32[128,128]{1,0:T(8,128)S(1)} %fusion.70) | copy-start | bytes 196612
  412.1 39.0 %copy-start.25 = (f32[256,128]{1,0:T(8,128)}, f32[256,128]{1,0:T(8,128)S(1)}, u32[]{:S(2)}) copy-start(f32[256,128]{1,0:T(8,128)S(1)} %get-tuple-element.72) | copy-start | bytes 393220
  420.7 30.5 %copy-start.22 = (f32[256,256]{1,0:T(8,128)}, f32[256,256]{1,0:T(8,128)S(1)}, u32[]{:S(2)}) copy-start(f32[256,256]{1,0:T(8,128)S(1)} %convolution_subtract_fusion.11) | copy-start | bytes 786436
  451.1 10.4 %copy-start.31 = (f32[128,128]{1,0:T(8,128)}, f32[128,128]{1,0:T(8,128)S(1)}, u32[]{:S(2)}) copy-start(f32[128,128]{1,0:T(8,128)S(1)} %fusion.64) | copy-start | bytes 196612
  452.0 9.6 %copy-start.39 = (f32[128,128]{1,0:T(8,128)}, f32[128,128]{1,0:T(8,128)S(1)}, u32[]{:S(2)}) copy-start(f32[128,128]{1,0:T(8,128)S(1)} %get-tuple-element.74) | copy-start | bytes 196612
  452.0 16.8 %copy-start.8 = (f32[896,128]{1,0:T(8,128)S(1)}, f32[896,128]{1,0:T(8,128)}, u32[]{:S(2)}) copy-start(f32[896,128]{1,0:T(8,128)} %copy-done.6) | copy-start | bytes 1376260
  468.8 4.9 copy-start.21
  520.7 5.1 copy-start.30
  542.9 6.4 %copy-start.1 = (f32[4,256,4,128]{1,3,2,0:T(8,128)S(1)}, f32[4,256,4,128]{1,3,2,0:T(8,128)}, u32[]{:S(2)}) copy-start(f32[4,256,4,128]{1,3,2,0:T(8,128)} %copy-done) | copy-start | bytes 6291460
  551.0 8.0 %copy-start.4 = (f32[1,4,256,4,128]{2,4,3,1,0:T(8,128)S(1)}, f32[1,4,256,4,128]{2,4,3,1,0:T(8,128)}, u32[]{:S(2)}) copy-start(f32[1,4,256,4,128]{2,4,3,1,0:T(8,128)} %get-tuple-element.58) | copy-start | bytes 6291460
  553.9 21.8 %all-to-all-start.10 = ((f32[8,3,32,3,128]{4,2,3,1,0:T(8,128)}), f32[8,3,32,3,128]{4,2,3,1,0:T(8,128)S(1)}, u32[]{:S(2)}, u32[]{:S(2)}) async-start(f32[8,3,32,3,128]{4,2,3,1,0:T(8,128)} %copy.91), calls=%async_computation.10 | async-start | bytes 2359296 | tf_op jit(solution)/shard_map/all_to_all | solution.py:72
  (25 other events, 62.0 us)
Sparse Core Ops, SparseCore 0:
  174.8 41.3 all-gather.2
